TPU v7x, 32 devices: a whole 2x2x4 slice. The times are simulated.
32 devices in a mesh: row: 8 (over z, y), col: 4 (over x, core).
Axes of the slice: x: 2, y: 2, z: 4, core: 2. Of those that a mesh axis runs over, the one named last changes fastest.
Arguments:
- inputs: bfloat16 [128, 8192], P('row', 'col'), may hold values from -6 to 6
- out_grad: bfloat16 [128, 8192], P('row', 'col'), may hold values from -96 to 96
- gate_weight: bfloat16 [8192, 16384], P('col', 'row'), may hold values from -0.0625 to 0.0625
- up_weight: bfloat16 [8192, 16384], P('col', 'row'), may hold values from -0.0625 to 0.0625
- down_weight: bfloat16 [16384, 8192], P('row', 'col'), may hold values from -0.046875 to 0.046875
Outputs:
- input_grad: bfloat16 [128, 8192], P('row', 'col')
- gate_grad: bfloat16 [8192, 16384], P('col', 'row')
- up_grad: bfloat16 [8192, 16384], P('col', 'row')
- down_grad: bfloat16 [16384, 8192], P('row', 'col')
All inputs are finite; a program needn't handle non-finite values.
Results may differ from a plain program's by a relative error of at most 0.005.
Values may be sent and summed in bfloat16 or wider, within the bound.
No kernel may reach another device: no remote copies, remote signals or barrier semaphores. Data moves between devices by JAX's collectives and lax.ppermute only.
A program may use at most 128 MiB of HBM per device.

v0:
```python
import jax
import jax.numpy as jnp
from jax import lax
from jax.sharding import PartitionSpec as P

LAYERS = 128


def contract_rows(left, right):
    return lax.dot_general(
        left, right, (((0,), (0,)), ((), ())), preferred_element_type=jnp.float32
    )


def contract_cols(left, right):
    return lax.dot_general(
        left, right, (((1,), (1,)), ((), ())), preferred_element_type=jnp.float32
    )


def gated_parts(gate, up, back, mult):
    sig = jax.nn.sigmoid(gate)
    hidden_grad = mult * back
    hidden = (gate * sig * up).astype(jnp.bfloat16)
    gate_delta = (hidden_grad * up * sig * (1.0 + gate * (1.0 - sig))).astype(jnp.bfloat16)
    up_delta = (hidden_grad * gate * sig).astype(jnp.bfloat16)
    return (hidden, gate_delta, up_delta)


def per_device(inputs, out_grad, gate_weight, up_weight, down_weight):
    mult = (2.0 * LAYERS) ** (-0.5)
    tokens_all = lax.all_gather(inputs, "row", axis=0, tiled=True)
    grads_all = lax.all_gather(out_grad, "row", axis=0, tiled=True)
    gate_part = jnp.dot(tokens_all, gate_weight, preferred_element_type=jnp.float32)
    up_part = jnp.dot(tokens_all, up_weight, preferred_element_type=jnp.float32)
    back_part = contract_cols(grads_all, down_weight)
    gate, up, back = lax.psum((gate_part, up_part, back_part), "col")
    hidden, gate_delta, up_delta = gated_parts(gate, up, back, mult)
    down_grad = (mult * contract_rows(hidden, grads_all)).astype(jnp.bfloat16)
    gate_grad = contract_rows(tokens_all, gate_delta).astype(jnp.bfloat16)
    up_grad = contract_rows(tokens_all, up_delta).astype(jnp.bfloat16)
    input_part = contract_cols(gate_delta, gate_weight) + contract_cols(up_delta, up_weight)
    input_grad = lax.psum_scatter(input_part, "row", scatter_dimension=0, tiled=True).astype(
        jnp.bfloat16
    )
    return (input_grad, gate_grad, up_grad, down_grad)


def solution(mesh):
    return jax.shard_map(
        per_device,
        mesh=mesh,
        in_specs=(
            P("row", "col"),
            P("row", "col"),
            P("col", "row"),
            P("col", "row"),
            P("row", "col"),
        ),
        out_specs=(P("row", "col"), P("col", "row"), P("col", "row"), P("row", "col")),
        check_vma=False,
    )
```

profile of v0, /device:TPU:0, one launch (start us, length us, event | category | flops | bytes accessed | tf_op | source)
XLA Modules:
  0.0 242.4 jit_solution(15786650038856876526)
XLA Ops:
  7.2 0.0 all-reduce.3.cloned.1.call-start
  7.2 0.0 slice-start
  7.2 33.4 %all_gather.7 = bf16[128,2048]{1,0:T(8,128)(2,1)S(1)} all-gather(bf16[16,2048]{1,0:T(8,128)(2,1)} %param.5), channel_id=1, replica_groups=mesh['row'=8,'col'=4] {'row'}, dimensions={0}, use_global_device_ids=true | all-gather | bytes 589824 | tf_op jit(solution)/shard_map/all_gather | solution.py:32
  40.6 0.0 slice-start.1
  40.6 0.0 slice-start.2
  40.6 5.8 %fusion.4 = f32[128,2048]{1,0:T(8,128)} fusion(bf16[128,2048]{1,0:T(8,128)(2,1)S(1)} %all_gather.7, bf16[2048,2048]{1,0:T(8,128)(2,1)} %param.7), kind=kOutput, calls=%fused_computation.12 | convolution fusion | flops 1073741824 | bytes 9961472 | tf_op jit(solution)/shard_map/dot_general | solution.py:34
  46.4 0.0 slice-done
  46.4 0.0 slice-done.1
  46.4 0.0 copy-start.2
  46.4 0.0 slice-start.3
  46.4 2.3 fusion.3
  48.7 0.0 copy-done.2
  48.7 31.3 %all_gather.6 = bf16[128,2048]{1,0:T(8,128)(2,1)S(1)} all-gather(bf16[16,2048]{1,0:T(8,128)(2,1)S(1)} %copy-done.2), channel_id=1, replica_groups=mesh['row'=8,'col'=4] {'row'}, dimensions={0}, use_global_device_ids=true | all-gather | bytes 589824 | tf_op jit(solution)/shard_map/all_gather | solution.py:33
  79.9 0.0 slice-done.2
  79.9 0.0 slice-done.3
  79.9 3.9 %fusion.2 = f32[128,2048]{1,0:T(8,128)} fusion(bf16[128,2048]{1,0:T(8,128)(2,1)S(1)} %all_gather.6, bf16[2048,2048]{1,0:T(8,128)(2,1)S(1)} %bitcast.22), kind=kOutput, calls=%fused_computation.10 | convolution fusion | flops 1073741824 | bytes 9961472 | tf_op jit(solution)/shard_map/dot_general | solution.py:16
  83.8 0.0 all-reduce.3.cloned.1.call-update
  83.8 0.2 reduce-scatter.2.cloned.1.call-start
  84.1 69.6 %all-reduce.3.cloned.1.call-done = (f32[128,2048]{1,0:T(8,128)}, f32[128,2048]{1,0:T(8,128)}, f32[128,2048]{1,0:T(8,128)}) async-done(((f32[128,2048]{1,0:T(8,128)}, f32[128,2048]{1,0:T(8,128)}, f32[128,2048]{1,0:T(8,128)}), (f32[128,2048]{1,0:T(8,128)}, f32[128,2048]{1,0:T(8,128)}, f32[128,2048]{1,0:T(8,128)})) %all-reduce.3.cloned.1.call-update) | async-done | bytes 3145744 | tf_op jit(solution)/shard_map/psum | solution.py:37
  153.7 2.3 multiply_convert_fusion.2
  156.0 6.3 %fusion.5 = f32[128,2048]{1,0:T(8,128)S(1)} fusion(bf16[128,2048]{1,0:T(8,128)(2,1)S(1)} %get-tuple-element.12, bf16[2048,2048]{1,0:T(8,128)(2,1)} %param.7), kind=kOutput, calls=%fused_computation.13 | convolution fusion | flops 1073741824 | bytes 9961472 | tf_op jit(solution)/shard_map/dot_general | solution.py:16
  162.3 7.3 %convolution_add_fusion = f32[128,2048]{1,0:T(8,128)} fusion(f32[128,2048]{1,0:T(8,128)S(1)} %fusion.5, bf16[128,2048]{1,0:T(8,128)(2,1)S(1)} %get-tuple-element.11, bf16[2048,2048]{1,0:T(8,128)(2,1)} %param.8), kind=kOutput, calls=%fused_computation.3 | convolution fusion | flops 1074003968 | bytes 11010048 | tf_op jit(solution)/shard_map/dot_general | solution.py:16
  169.5 0.0 reduce-scatter.2.cloned.1.call-update
  169.6 5.8 %convert_bitcast_fusion.1 = bf16[2048,2048]{0,1:T(8,128)(2,1)} fusion(bf16[128,2048]{1,0:T(8,128)(2,1)S(1)} %get-tuple-element.12, bf16[128,2048]{1,0:T(8,128)(2,1)S(1)} %all_gather.7), kind=kOutput, calls=%fused_computation.2 | convolution fusion | flops 1077936128 | bytes 9437184 | tf_op jit(solution)/shard_map/dot_general | solution.py:10
  175.3 12.2 %copy.9 = bf16[2048,2048]{1,0:T(8,128)(2,1)} copy(bf16[2048,2048]{0,1:T(8,128)(2,1)} %convert_bitcast_fusion.1) | data formatting | bytes 16777216
  187.6 5.8 %convert_bitcast_fusion = bf16[2048,2048]{0,1:T(8,128)(2,1)} fusion(bf16[128,2048]{1,0:T(8,128)(2,1)S(1)} %get-tuple-element.11, bf16[128,2048]{1,0:T(8,128)(2,1)S(1)} %all_gather.7), kind=kOutput, calls=%fused_computation.1 | convolution fusion | flops 1077936128 | bytes 9437184 | tf_op jit(solution)/shard_map/dot_general | solution.py:10
  193.3 0.0 copy-start
  193.3 0.0 copy-start.1
  193.3 12.4 %copy.10 = bf16[2048,2048]{1,0:T(8,128)(2,1)} copy(bf16[2048,2048]{0,1:T(8,128)(2,1)} %convert_bitcast_fusion) | data formatting | bytes 16777216
  205.7 0.0 copy-done
  205.7 0.0 copy-done.1
  205.7 5.8 %multiply_convert_fusion = bf16[2048,2048]{1,0:T(8,128)(2,1)} fusion(bf16[128,2048]{1,0:T(8,128)(2,1)S(1)} %all_gather.6, f32[128,2048]{1,0:T(8,128)S(1)} %copy-done.1, f32[128,2048]{1,0:T(8,128)S(1)} %copy-done), kind=kOutput, calls=%fused_computation | convolution fusion | flops 1083703296 | bytes 11010048 | tf_op jit(solution)/shard_map/dot_general | solution.py:10
  211.5 22.4 %reduce-scatter.2.cloned.1.call-done = f32[16,2048]{1,0:T(8,128)} async-done(((f32[128,2048]{1,0:T(8,128)}), f32[16,2048]{1,0:T(8,128)}) %reduce-scatter.2.cloned.1.call-update) | async-done | bytes 131088 | tf_op jit(solution)/shard_map/reduce_scatter | solution.py:43
  234.0 1.5 convert_element_type.29
  (2 shorter events, 0.0 us)
Async XLA Ops:
  7.2 146.5 %all-reduce.3.cloned.1.call-start = ((), (), s32[]{:S(2)}) async-start(), calls=%async_computation.2 | async-start | bytes 6291456 | tf_op jit(solution)/shard_map/psum | solution.py:37
  7.2 39.2 %slice-start = ((s8[8388608]{0:T(1024)(128)(4,1)}), s8[4194304]{0:T(1024)(128)(4,1)S(1)}, s32[]{:S(2)}) async-start(s8[8388608]{0:T(1024)(128)(4,1)} %bitcast.19), calls=%async_computation.3 | async-start | bytes 8388608
  40.6 5.8 %slice-start.1 = ((s8[8388608]{0:T(1024)(128)(4,1)}), s8[4194304]{0:T(1024)(128)(4,1)S(1)}, s32[]{:S(2)}) async-start(s8[8388608]{0:T(1024)(128)(4,1)} %bitcast.19), calls=%async_computation.4 | async-start | bytes 8388608
  40.6 39.3 %slice-start.2 = ((s8[8388608]{0:T(1024)(128)(4,1)}), s8[4194304]{0:T(1024)(128)(4,1)S(1)}, s32[]{:S(2)}) async-start(s8[8388608]{0:T(1024)(128)(4,1)} %bitcast.21), calls=%async_computation.5 | async-start | bytes 8388608
  46.4 2.3 copy-start.2
  46.4 33.6 %slice-start.3 = ((s8[8388608]{0:T(1024)(128)(4,1)}), s8[4194304]{0:T(1024)(128)(4,1)S(1)}, s32[]{:S(2)}) async-start(s8[8388608]{0:T(1024)(128)(4,1)} %bitcast.21), calls=%async_computation.6 | async-start | bytes 8388608
  83.8 150.2 %reduce-scatter.2.cloned.1.call-start = ((), (), s32[]{:S(2)}) async-start(), calls=%async_computation.1 | async-start | bytes 1179648 | tf_op jit(solution)/shard_map/reduce_scatter | solution.py:43
  193.3 12.4 %copy-start = (f32[128,2048]{1,0:T(8,128)S(1)}, f32[128,2048]{1,0:T(8,128)}, u32[]{:S(2)}) copy-start(f32[128,2048]{1,0:T(8,128)} %get-tuple-element.8) | copy-start | bytes 3145732
  193.3 12.4 %copy-start.1 = (f32[128,2048]{1,0:T(8,128)S(1)}, f32[128,2048]{1,0:T(8,128)}, u32[]{:S(2)}) copy-start(f32[128,2048]{1,0:T(8,128)} %get-tuple-element.9) | copy-start | bytes 3145732
Sparse Core Ops, SparseCore 0:
  83.9 69.6 all-reduce.2
  169.7 64.2 reduce-scatter.1
where the time goes:
time: 243 us; the launch traced here: 242 us
  waiting for transfers between devices  92.1 us (38%)
  blocking collectives  64.6 us (27%)
  matrix products  42.8 us (18%)
  local copies, waits for them, and re-layouts  24.7 us (10%)
  between operations  14.1 us (6%)
  other arithmetic  3.89 us (2%)
    psum x1, waiting for transfers between devices, per_device(): gate, up, back = lax.psum((gate_part, up_part, back_part), 'col')  69.6 us
    all_gather x1, blocking collectives, per_device(): tokens_all = lax.all_gather(inputs, 'row', axis=0, tiled=True)  33.4 us
    all_gather x1, blocking collectives, per_device(): grads_all = lax.all_gather(out_grad, 'row', axis=0, tiled=True)  31.3 us
    unnamed x16, local copies, waits for them, and re-layouts  24.7 us
    reduce_scatter x1, waiting for transfers between devices, per_device(): lax.psum_scatter(input_part, 'row', scatter_dimension=0, tiled=True)  22.4 us
    dot_general x3, matrix products, contract_cols(): lax.dot_general(left, right, (((1,), (1,)), ((), ())), preferred_element_...  17.4 us
    dot_general x3, matrix products, contract_rows(): lax.dot_general(left, right, (((0,), (0,)), ((), ())), preferred_element_...  17.3 us
    dot_general x1, matrix products, per_device(): jnp.dot(tokens_all, gate_weight, preferred_element_type=jnp.float32)  5.76 us
  transfers between devices with their start and end apart: 2, of which 2 were waited for; matrix products, arithmetic and copies ran while one was open for 17% of the time, Pallas kernels for 0%

commit v1 on v0

--- a/solution.py
+++ b/solution.py
@@ -29,7 +29,12 @@
 
 def per_device(inputs, out_grad, gate_weight, up_weight, down_weight):
     mult = (2.0 * LAYERS) ** (-0.5)
-    tokens_all = lax.all_gather(inputs, "row", axis=0, tiled=True)
+    ring = [inputs]
+    for hop in range(7):
+        ring.append(lax.ppermute(ring[-1], "row", [(dev, (dev + 1) % 8) for dev in range(8)]))
+    tokens_all = jnp.roll(
+        jnp.concatenate(ring[::-1], axis=0), (lax.axis_index("row") + 1) * ring[0].shape[0], axis=0
+    )
     grads_all = lax.all_gather(out_grad, "row", axis=0, tiled=True)
     gate_part = jnp.dot(tokens_all, gate_weight, preferred_element_type=jnp.float32)
     up_part = jnp.dot(tokens_all, up_weight, preferred_element_type=jnp.float32)

time: 243 us -> 251 us (1.033)
  waiting for transfers between devices: 92.1 us -> 149 us
  blocking collectives: 64.6 us -> 31.7 us
  local copies, waits for them, and re-layouts: 24.7 us -> 0.13 us
  starting transfers between devices: 0.26 us -> 5.24 us
  matrix products: 42.8 us -> 46.1 us
    ppermute x0 -> x7, waiting for transfers between devices: none -> 33.7 us  [per_device(): lax.ppermute(ring[-1], 'row', [(dev, (dev + 1) % 8) for dev in range(8)])]
    all_gather x1 -> x0, blocking collectives: 33.4 us -> none  [per_device(): tokens_all = lax.all_gather(inputs, 'row', axis=0, tiled=True)]
    reduce_scatter x1, waiting for transfers between devices: 22.4 us -> 47 us  [per_device(): lax.psum_scatter(input_part, 'row', scatter_dimension=0, tiled=True)]
    unnamed x16 -> x25, local copies, waits for them, and re-layouts: 24.7 us -> 0.13 us
    ppermute x0 -> x7, starting transfers between devices: none -> 4.98 us  [per_device(): lax.ppermute(ring[-1], 'row', [(dev, (dev + 1) % 8) for dev in range(8)])]
    dot_general x3, matrix products: 17.4 us -> 20.7 us  [contract_cols(): lax.dot_general(left, right, (((1,), (1,)), ((), ())), preferred_element_...]
  transfers between devices with their start and end apart: 2 -> 9, of which waited for: 2 -> 7; matrix products, arithmetic and copies ran while one was open for 17% -> 10% of each run, Pallas kernels for 0% -> 0%
where the time goes in v1:
time: 251 us
  waiting for transfers between devices  149 us (59%)
  matrix products  46.1 us (18%)
  blocking collectives  31.7 us (13%)
  between operations  14.2 us (6%)
  starting transfers between devices  5.24 us (2%)
  other arithmetic  3.88 us (2%)
    psum x1, waiting for transfers between devices, per_device(): gate, up, back = lax.psum((gate_part, up_part, back_part), 'col')  68.6 us
    reduce_scatter x1, waiting for transfers between devices, per_device(): lax.psum_scatter(input_part, 'row', scatter_dimension=0, tiled=True)  47 us
    ppermute x7, waiting for transfers between devices, per_device(): lax.ppermute(ring[-1], 'row', [(dev, (dev + 1) % 8) for dev in range(8)])  33.7 us
    all_gather x1, blocking collectives, per_device(): grads_all = lax.all_gather(out_grad, 'row', axis=0, tiled=True)  31.7 us
    dot_general x3, matrix products, contract_cols(): lax.dot_general(left, right, (((1,), (1,)), ((), ())), preferred_element_...  20.7 us
    dot_general x3, matrix products, contract_rows(): lax.dot_general(left, right, (((0,), (0,)), ((), ())), preferred_element_...  17.4 us
    dot_general x1, matrix products, per_device(): jnp.dot(tokens_all, gate_weight, preferred_element_type=jnp.float32)  5.76 us
  transfers between devices with their start and end apart: 9, of which 7 were waited for; matrix products, arithmetic and copies ran while one was open for 10% of the time, Pallas kernels for 0%

profile of v1, /device:TPU:0, one launch (start us, length us, event | category | flops | bytes accessed | tf_op | source)
XLA Modules:
  0.0 250.6 jit_solution(9769457856488640433)
XLA Ops:
  7.2 0.0 copy-start.2
  7.2 0.0 all-reduce.3.cloned.1.call-start
  7.2 3.0 %collective-permute-start = (bf16[16,2048]{1,0:T(8,128)(2,1)}, bf16[16,2048]{1,0:T(8,128)(2,1)S(1)}, u32[]{:S(2)}, u32[]{:S(2)}) collective-permute-start(bf16[16,2048]{1,0:T(8,128)(2,1)} %param.5), channel_id=1, source_target_pairs={{0,4},{4,8},{8,12},{12,16},{16,20},{20,24},{24,28},{28,0},{1,5},{5... | collective-permute-start | bytes 196616 | tf_op jit(solution)/shard_map/ppermute | solution.py:34
  10.3 5.5 %collective-permute-done = bf16[16,2048]{1,0:T(8,128)(2,1)S(1)} collective-permute-done((bf16[16,2048]{1,0:T(8,128)(2,1)}, bf16[16,2048]{1,0:T(8,128)(2,1)S(1)}, u32[]{:S(2)}, u32[]{:S(2)}) %collective-permute-start) | collective-permute-done | bytes 65568 | tf_op jit(solution)/shard_map/ppermute | solution.py:34
  15.8 0.0 collective-permute-start.1
  15.8 7.0 %collective-permute-done.1 = bf16[16,2048]{1,0:T(8,128)(2,1)S(1)} collective-permute-done((bf16[16,2048]{1,0:T(8,128)(2,1)S(1)}, bf16[16,2048]{1,0:T(8,128)(2,1)S(1)}, u32[]{:S(2)}, u32[]{:S(2)}) %collective-permute-start.1) | collective-permute-done | bytes 65568 | tf_op jit(solution)/shard_map/ppermute | solution.py:34
  22.7 0.0 collective-permute-start.2
  22.7 7.0 %collective-permute-done.2 = bf16[16,2048]{1,0:T(8,128)(2,1)S(1)} collective-permute-done((bf16[16,2048]{1,0:T(8,128)(2,1)S(1)}, bf16[16,2048]{1,0:T(8,128)(2,1)S(1)}, u32[]{:S(2)}, u32[]{:S(2)}) %collective-permute-start.2) | collective-permute-done | bytes 65568 | tf_op jit(solution)/shard_map/ppermute | solution.py:34
  29.7 0.0 collective-permute-start.3
  29.7 7.0 %collective-permute-done.3 = bf16[16,2048]{1,0:T(8,128)(2,1)S(1)} collective-permute-done((bf16[16,2048]{1,0:T(8,128)(2,1)S(1)}, bf16[16,2048]{1,0:T(8,128)(2,1)S(1)}, u32[]{:S(2)}, u32[]{:S(2)}) %collective-permute-start.3) | collective-permute-done | bytes 65568 | tf_op jit(solution)/shard_map/ppermute | solution.py:34
  36.7 0.0 collective-permute-start.4
  36.7 7.3 %collective-permute-done.4 = bf16[16,2048]{1,0:T(8,128)(2,1)S(1)} collective-permute-done((bf16[16,2048]{1,0:T(8,128)(2,1)S(1)}, bf16[16,2048]{1,0:T(8,128)(2,1)S(1)}, u32[]{:S(2)}, u32[]{:S(2)}) %collective-permute-start.4) | collective-permute-done | bytes 65568 | tf_op jit(solution)/shard_map/ppermute | solution.py:34
  44.0 0.0 collective-permute-start.5
  44.0 31.7 %all_gather.3 = bf16[128,2048]{1,0:T(8,128)(2,1)S(1)} all-gather(bf16[16,2048]{1,0:T(8,128)(2,1)} %param.6), channel_id=1, replica_groups=mesh['row'=8,'col'=4] {'row'}, dimensions={0}, use_global_device_ids=true | all-gather | bytes 589824 | tf_op jit(solution)/shard_map/all_gather | solution.py:38
  75.6 0.0 collective-permute-done.5
  75.6 1.9 collective-permute-start.6
  77.6 7.2 %fusion.12 = f32[128,2048]{1,0:T(8,128)} fusion(bf16[128,2048]{1,0:T(8,128)(2,1)S(1)} %all_gather.3, bf16[2048,2048]{1,0:T(8,128)(2,1)} %param.9), kind=kOutput, calls=%fused_computation.36 | convolution fusion | flops 1073741824 | bytes 9961472 | tf_op jit(solution)/shard_map/dot_general | solution.py:16
  84.8 0.0 collective-permute-done.6
  84.8 0.0 slice-start
  84.9 0.0 copy-done.2
  85.0 0.0 slice-start.1
  85.1 5.8 %fusion.3 = f32[128,2048]{1,0:T(8,128)} fusion(bf16[2048,2048]{1,0:T(8,128)(2,1)} %param.7, bf16[256,2048]{1,0:T(8,128)(2,1)S(1)} %constant_dynamic-update-slice_fusion, s32[]{:T(128)S(6)} %select_n.14), kind=kOutput, calls=%fused_computation.11 | convolution fusion | flops 1073741824 | bytes 9961476 | tf_op jit(solution)/shard_map/dot_general | solution.py:39
  90.8 0.0 slice-done
  90.8 0.0 slice-done.1
  90.8 2.3 fusion.5
  93.1 0.0 all-reduce.3.cloned.1.call-update
  93.1 0.2 reduce-scatter.2.cloned.1.call-start
  93.4 68.6 %all-reduce.3.cloned.1.call-done = (f32[128,2048]{1,0:T(8,128)}, f32[128,2048]{1,0:T(8,128)}, f32[128,2048]{1,0:T(8,128)}) async-done(((f32[128,2048]{1,0:T(8,128)}, f32[128,2048]{1,0:T(8,128)}, f32[128,2048]{1,0:T(8,128)}), (f32[128,2048]{1,0:T(8,128)}, f32[128,2048]{1,0:T(8,128)}, f32[128,2048]{1,0:T(8,128)})) %all-reduce.3.cloned.1.call-update) | async-done | bytes 3145744 | tf_op jit(solution)/shard_map/psum | solution.py:42
  162.0 2.3 multiply_convert_fusion.2
  164.3 6.3 %fusion.13 = f32[128,2048]{1,0:T(8,128)S(1)} fusion(bf16[128,2048]{1,0:T(8,128)(2,1)S(1)} %get-tuple-element.8, bf16[2048,2048]{1,0:T(8,128)(2,1)} %param.7), kind=kOutput, calls=%fused_computation.37 | convolution fusion | flops 1073741824 | bytes 9961472 | tf_op jit(solution)/shard_map/dot_general | solution.py:16
  170.6 7.3 %convolution_add_fusion = f32[128,2048]{1,0:T(8,128)} fusion(f32[128,2048]{1,0:T(8,128)S(1)} %fusion.13, bf16[128,2048]{1,0:T(8,128)(2,1)S(1)} %get-tuple-element.7, bf16[2048,2048]{1,0:T(8,128)(2,1)} %param.8), kind=kOutput, calls=%fused_computation.3 | convolution fusion | flops 1074003968 | bytes 11010048 | tf_op jit(solution)/shard_map/dot_general | solution.py:16
  177.8 0.0 reduce-scatter.2.cloned.1.call-update
  177.9 5.8 %convolution_convert_fusion = bf16[2048,2048]{1,0:T(8,128)(2,1)} fusion(bf16[128,2048]{1,0:T(8,128)(2,1)S(1)} %get-tuple-element.7, bf16[256,2048]{1,0:T(8,128)(2,1)S(1)} %constant_dynamic-update-slice_fusion, s32[]{:T(128)S(6)} %select_n.14), kind=kOutput, calls=%fused_computation.1 | convolution fusion | flops 1077936128 | bytes 9437188 | tf_op jit(solution)/shard_map/dot_general | solution.py:10
  183.6 0.0 copy-start
  183.6 0.0 copy-start.1
  183.6 5.8 %convolution_convert_fusion.1 = bf16[2048,2048]{1,0:T(8,128)(2,1)} fusion(bf16[128,2048]{1,0:T(8,128)(2,1)S(1)} %get-tuple-element.8, bf16[256,2048]{1,0:T(8,128)(2,1)S(1)} %constant_dynamic-update-slice_fusion, s32[]{:T(128)S(6)} %select_n.14), kind=kOutput, calls=%fused_computation.2 | convolution fusion | flops 1077936128 | bytes 9437188 | tf_op jit(solution)/shard_map/dot_general | solution.py:10
  189.4 0.0 copy-done
  189.4 0.0 copy-done.1
  189.4 5.8 %multiply_convert_fusion = bf16[2048,2048]{1,0:T(8,128)(2,1)} fusion(bf16[128,2048]{1,0:T(8,128)(2,1)S(1)} %all_gather.3, f32[128,2048]{1,0:T(8,128)S(1)} %copy-done.1, f32[128,2048]{1,0:T(8,128)S(1)} %copy-done), kind=kOutput, calls=%fused_computation | convolution fusion | flops 1083703296 | bytes 11010048 | tf_op jit(solution)/shard_map/dot_general | solution.py:10
  195.2 47.0 %reduce-scatter.2.cloned.1.call-done = f32[16,2048]{1,0:T(8,128)} async-done(((f32[128,2048]{1,0:T(8,128)}), f32[16,2048]{1,0:T(8,128)}) %reduce-scatter.2.cloned.1.call-update) | async-done | bytes 131088 | tf_op jit(solution)/shard_map/reduce_scatter | solution.py:48
  242.3 1.5 convert_element_type.23
  (17 shorter events, 0.1 us)
Async XLA Ops:
  7.2 77.7 %copy-start.2 = (bf16[16,2048]{1,0:T(8,128)(2,1)S(1)}, bf16[16,2048]{1,0:T(8,128)(2,1)}, u32[]{:S(2)}) copy-start(bf16[16,2048]{1,0:T(8,128)(2,1)} %param.5) | copy-start | bytes 196612
  7.2 154.8 %all-reduce.3.cloned.1.call-start = ((), (), s32[]{:S(2)}) async-start(), calls=%async_computation.2 | async-start | bytes 6291456 | tf_op jit(solution)/shard_map/psum | solution.py:42
  7.2 8.5 %collective-permute-start = (bf16[16,2048]{1,0:T(8,128)(2,1)}, bf16[16,2048]{1,0:T(8,128)(2,1)S(1)}, u32[]{:S(2)}, u32[]{:S(2)}) collective-permute-start(bf16[16,2048]{1,0:T(8,128)(2,1)} %param.5), channel_id=1, source_target_pairs={{0,4},{4,8},{8,12},{12,16},{16,20},{20,24},{24,28},{28,0},{1,5},{5... | collective-permute-start | bytes 196616 | tf_op jit(solution)/shard_map/ppermute | solution.py:34
  15.8 7.0 %collective-permute-start.1 = (bf16[16,2048]{1,0:T(8,128)(2,1)S(1)}, bf16[16,2048]{1,0:T(8,128)(2,1)S(1)}, u32[]{:S(2)}, u32[]{:S(2)}) collective-permute-start(bf16[16,2048]{1,0:T(8,128)(2,1)S(1)} %collective-permute-done), channel_id=1, source_target_pairs={{0,4},{4,8},{8,12},{12,16},{16,20},{20,24},{24,28},{28,0},{1,5},{5... | collective-permute-start | bytes 196616 | tf_op jit(solution)/shard_map/ppermute | solution.py:34
  22.7 7.0 %collective-permute-start.2 = (bf16[16,2048]{1,0:T(8,128)(2,1)S(1)}, bf16[16,2048]{1,0:T(8,128)(2,1)S(1)}, u32[]{:S(2)}, u32[]{:S(2)}) collective-permute-start(bf16[16,2048]{1,0:T(8,128)(2,1)S(1)} %collective-permute-done.1), channel_id=1, source_target_pairs={{0,4},{4,8},{8,12},{12,16},{16,20},{20,24},{24,28},{28,0},{1,5},{5... | collective-permute-start | bytes 196616 | tf_op jit(solution)/shard_map/ppermute | solution.py:34
  29.7 7.0 %collective-permute-start.3 = (bf16[16,2048]{1,0:T(8,128)(2,1)S(1)}, bf16[16,2048]{1,0:T(8,128)(2,1)S(1)}, u32[]{:S(2)}, u32[]{:S(2)}) collective-permute-start(bf16[16,2048]{1,0:T(8,128)(2,1)S(1)} %collective-permute-done.2), channel_id=1, source_target_pairs={{0,4},{4,8},{8,12},{12,16},{16,20},{20,24},{24,28},{28,0},{1,5},{5... | collective-permute-start | bytes 196616 | tf_op jit(solution)/shard_map/ppermute | solution.py:34
  36.7 7.3 %collective-permute-start.4 = (bf16[16,2048]{1,0:T(8,128)(2,1)S(1)}, bf16[16,2048]{1,0:T(8,128)(2,1)S(1)}, u32[]{:S(2)}, u32[]{:S(2)}) collective-permute-start(bf16[16,2048]{1,0:T(8,128)(2,1)S(1)} %collective-permute-done.3), channel_id=1, source_target_pairs={{0,4},{4,8},{8,12},{12,16},{16,20},{20,24},{24,28},{28,0},{1,5},{5... | collective-permute-start | bytes 196616 | tf_op jit(solution)/shard_map/ppermute | solution.py:34
  44.0 31.7 %collective-permute-start.5 = (bf16[16,2048]{1,0:T(8,128)(2,1)S(1)}, bf16[16,2048]{1,0:T(8,128)(2,1)S(1)}, u32[]{:S(2)}, u32[]{:S(2)}) collective-permute-start(bf16[16,2048]{1,0:T(8,128)(2,1)S(1)} %collective-permute-done.4), channel_id=1, source_target_pairs={{0,4},{4,8},{8,12},{12,16},{16,20},{20,24},{24,28},{28,0},{1,5},{5... | collective-permute-start | bytes 196616 | tf_op jit(solution)/shard_map/ppermute | solution.py:34
  75.6 9.1 %collective-permute-start.6 = (bf16[16,2048]{1,0:T(8,128)(2,1)S(1)}, bf16[16,2048]{1,0:T(8,128)(2,1)S(1)}, u32[]{:S(2)}, u32[]{:S(2)}) collective-permute-start(bf16[16,2048]{1,0:T(8,128)(2,1)S(1)} %collective-permute-done.5), channel_id=1, source_target_pairs={{0,4},{4,8},{8,12},{12,16},{16,20},{20,24},{24,28},{28,0},{1,5},{5... | collective-permute-start | bytes 196616 | tf_op jit(solution)/shard_map/ppermute | solution.py:34
  84.8 6.0 %slice-start = ((s8[8388608]{0:T(1024)(128)(4,1)}), s8[4194304]{0:T(1024)(128)(4,1)S(1)}, s32[]{:S(2)}) async-start(s8[8388608]{0:T(1024)(128)(4,1)} %bitcast.11), calls=%async_computation.3 | async-start | bytes 8388608
  85.0 5.8 %slice-start.1 = ((s8[8388608]{0:T(1024)(128)(4,1)}), s8[4194304]{0:T(1024)(128)(4,1)S(1)}, s32[]{:S(2)}) async-start(s8[8388608]{0:T(1024)(128)(4,1)} %bitcast.11), calls=%async_computation.4 | async-start | bytes 8388608
  93.1 149.1 %reduce-scatter.2.cloned.1.call-start = ((), (), s32[]{:S(2)}) async-start(), calls=%async_computation.1 | async-start | bytes 1179648 | tf_op jit(solution)/shard_map/reduce_scatter | solution.py:48
  183.6 5.8 %copy-start = (f32[128,2048]{1,0:T(8,128)S(1)}, f32[128,2048]{1,0:T(8,128)}, u32[]{:S(2)}) copy-start(f32[128,2048]{1,0:T(8,128)} %get-tuple-element.4) | copy-start | bytes 3145732
  183.6 5.8 %copy-start.1 = (f32[128,2048]{1,0:T(8,128)S(1)}, f32[128,2048]{1,0:T(8,128)}, u32[]{:S(2)}) copy-start(f32[128,2048]{1,0:T(8,128)} %get-tuple-element.5) | copy-start | bytes 3145732
Sparse Core Ops, SparseCore 0:
  93.2 68.6 all-reduce.2
  178.0 64.2 reduce-scatter.1
